TPU v7x, 128 devices: a whole 4x4x4 slice. The times are simulated.
128 devices in a mesh: row: 32 (over z, y, core), sub: 4 (over x).
Axes of the slice: x: 4, y: 4, z: 4, core: 2. Of those that a mesh axis runs over, the one named last changes fastest.
Arguments:
- images: bfloat16 [32768, 3072], P(('row', 'sub')), may hold values from -6 to 6
- block_id: int32 [128, 32], replicated, may hold values from 0 to 4095, as said below
- panel_index: int32 [1], replicated, may hold values from 0 to 30
Outputs:
- factor_panel: float32 [32768, 1024], P(('row', 'sub'))
- next_panel: float32 [32768, 1024], P(('row', 'sub'))
Inputs may be any that keep to these rules, and one draw needn't show every extreme that they name: `block_id`: column r holds r * 128 plus a permutation of 0 to 127, so every device stores exactly one block of every panel.
All inputs are finite; a program needn't handle non-finite values.
Results may differ from a plain program's by a relative error of at most 0.0015.
Values may be sent and summed in bfloat16 or wider, within the bound.
A program may use at most 128 MiB of HBM per device.

v0:
```python
import math

import jax
import jax.numpy as jnp
from jax import lax
from jax.sharding import PartitionSpec as P

PANEL = 1024
DEPTH = 10


weight_var = 2.0
bias_var = 0.1
noise_var = 0.1


def base_kernel(left, right):
    gram = lax.dot_general(
        left, right, (((1,), (1,)), ((), ())), preferred_element_type=jnp.float32
    )
    return gram * (weight_var / left.shape[1]) + bias_var


def row_variance(rows):
    values = rows.astype(jnp.float32)
    return jnp.sum(values * values, axis=1) * (weight_var / rows.shape[1]) + bias_var


def relu_layers(kernel, left_var, right_var):

    def one_layer(step_index, carried):
        current, lvar, rvar = carried
        scales = jnp.sqrt(lvar[:, None] * rvar[None, :])
        cosine = jnp.clip(current / scales, -1.0, 1.0)
        angles = jnp.arccos(cosine)
        current = (
            weight_var / (2.0 * math.pi) * scales * (jnp.sin(angles) + (math.pi - angles) * cosine)
            + bias_var
        )
        return (current, 0.5 * weight_var * lvar + bias_var, 0.5 * weight_var * rvar + bias_var)

    return lax.fori_loop(0, DEPTH, one_layer, (kernel, left_var, right_var))[0]


def product_nt(left, right):
    return lax.dot_general(
        left,
        right,
        (((1,), (1,)), ((), ())),
        precision=lax.Precision.HIGHEST,
        preferred_element_type=jnp.float32,
    )


def body(images, block_id, panel_index):
    rows_dev, features = images.shape
    shards = lax.axis_size("row") * lax.axis_size("sub")
    group_rows = PANEL // shards
    myself = lax.axis_index("row") * lax.axis_size("sub") + lax.axis_index("sub")
    panel = panel_index[0]
    local_rounds = jnp.arange(rows_dev, dtype=jnp.int32) // group_rows
    within = jnp.arange(rows_dev, dtype=jnp.int32) % group_rows
    columns = jnp.arange(PANEL, dtype=jnp.int32)
    identity = jnp.eye(PANEL, dtype=jnp.float32)
    local_var = row_variance(images)

    def arrangement(which):
        positions = lax.dynamic_index_in_dim(block_id, which, 1, keepdims=False) - which * shards
        sources = (
            jnp.zeros((shards,), jnp.int32).at[positions].set(jnp.arange(shards, dtype=jnp.int32))
        )
        return (sources, positions[myself])

    def reorder(blocks, sources):
        return blocks[sources].reshape(PANEL, -1)

    def own_mask(which, position):
        hits = (local_rounds == which)[:, None] & (
            columns[None, :] == position * group_rows + within[:, None]
        )
        return noise_var * hits.astype(jnp.float32)

    own_rows = lax.dynamic_slice_in_dim(images, panel * group_rows, 2 * group_rows, 0)
    gathered = lax.all_gather(own_rows, ("row", "sub"), axis=0, tiled=True)
    image_blocks = gathered.reshape(shards, 2, group_rows, features)
    sources, position = arrangement(panel)
    next_sources, next_position = arrangement(panel + 1)
    panel_images = reorder(image_blocks[:, 0], sources)
    next_images = reorder(image_blocks[:, 1], next_sources)
    panel_var = row_variance(panel_images)
    matrix = relu_layers(base_kernel(images, panel_images), local_var, panel_var) + own_mask(
        panel, position
    )
    pieces = []
    pieces.append(lax.dynamic_slice_in_dim(matrix, panel * group_rows, group_rows, 0))
    received = []
    outgoing = pieces[0]
    arrived = lax.all_gather(outgoing, ("row", "sub"), axis=0, tiled=True).reshape(
        shards, len(pieces), group_rows, PANEL
    )
    received = [arrived[:, 0]]
    diagonal_block = reorder(received[0], sources)
    lower = jnp.linalg.cholesky(diagonal_block)
    inverse_factor = jax.scipy.linalg.solve_triangular(lower, identity, lower=True)
    solved = product_nt(matrix, inverse_factor)
    own_lower = lax.dynamic_slice_in_dim(lower, position * group_rows, group_rows, 0)
    placed = lax.dynamic_update_slice_in_dim(
        jnp.zeros_like(solved), own_lower, panel * group_rows, 0
    )
    factor = jnp.where(
        (local_rounds > panel)[:, None],
        solved,
        jnp.where((local_rounds == panel)[:, None], placed, 0.0),
    )
    next_matrix = relu_layers(
        base_kernel(images, next_images), local_var, row_variance(next_images)
    ) + own_mask(panel + 1, next_position)
    next_rows = lax.dynamic_slice_in_dim(factor, (panel + 1) * group_rows, group_rows, 0)
    next_factor = reorder(
        lax.all_gather(next_rows, ("row", "sub"), axis=0, tiled=True).reshape(
            shards, group_rows, PANEL
        ),
        next_sources,
    )
    updated = next_matrix - product_nt(factor, next_factor)
    updated = jnp.where((local_rounds > panel)[:, None], updated, 0.0)
    return (factor, updated)


def solution(mesh):
    in_specs = (P(("row", "sub"), None), P(), P())
    out_specs = (P(("row", "sub"), None), P(("row", "sub"), None))
    return jax.shard_map(body, mesh=mesh, in_specs=in_specs, out_specs=out_specs, check_vma=False)
```

profile of v0, /device:TPU:1, one launch (start us, length us, event | category | flops | bytes accessed | tf_op | source)
XLA Modules:
  0.0 699.6 jit_solution(3645732903589708444)
XLA Ops:
  14.5 74.1 %all-gather.4.cloned.1.call-done = bf16[2048,3072]{1,0:T(8,128)(2,1)} async-done(((bf16[16,3072]{1,0:T(8,128)(2,1)}), bf16[2048,3072]{1,0:T(8,128)(2,1)}) %all-gather.4.cloned.1.call-update) | async-done | bytes 12582928 | tf_op jit(solution)/shard_map/all_gather | solution.py:84
  88.6 10.6 %slice_bitcast_fusion = (bf16[128,8,3072]{2,1,0:T(8,128)(2,1)}, bf16[128,8,3072]{2,1,0:T(8,128)(2,1)}) fusion(bf16[128,2,8,3072]{3,2,1,0:T(8,128)(2,1)} %bitcast.165), kind=kLoop, calls=%fused_computation.16 | loop fusion | bytes 25165824 | tf_op jit(solution)/shard_map/squeeze | solution.py:89
  114.8 61.0 %while.29 = (s32[]{:T(128)}, f32[256,1024]{1,0:T(8,128)S(1)}, f32[256]{0:T(256)S(1)}, f32[1024]{0:T(1024)S(1)}, s32[]{:T(128)}) while((s32[]{:T(128)}, f32[256,1024]{1,0:T(8,128)S(1)}, f32[256]{0:T(256)S(1)}, f32[1024]{0:T(1024)S(1)}, s32[]{:T(128)}) %tuple.114), condition=%wide.region_4.5_spmd, body=%wide.region_3.4_spmd.sunk | while | flops 3147010 | bytes 2112573 | solution.py:42
  196.3 46.9 %all-gather.6.cloned.1.call-done = f32[1024,1024]{1,0:T(8,128)} async-done(((f32[8,1024]{1,0:T(8,128)}), f32[1024,1024]{1,0:T(8,128)}) %all-gather.6.cloned.1.call-update) | async-done | bytes 4194320 | tf_op jit(solution)/shard_map/all_gather | solution.py:98
  260.2 11.7 %cholesky.223 = f32[128,128]{1,0:T(8,128)S(1)} custom-call(f32[128,128]{1,0:T(8,128)S(1)} %cholesky.580), custom_call_target="Cholesky" | custom-call | tf_op jit(solution)/shard_map/jit(cholesky)/cholesky | solution.py:103
  272.6 9.8 %custom-call.63 = f32[1,128,128]{1,2,0:T(8,128)S(1)} custom-call(f32[1,128,128]{2,1,0:T(8,128)S(1)} %get-tuple-element.152), custom_call_target="InvertDiagBlocksLowerTriangular" | custom-call | tf_op jit(solution)/shard_map/jit(cholesky)/cholesky | solution.py:103
  288.9 20.4 %cholesky.244 = f32[128,128]{1,0:T(8,128)S(1)} custom-call(f32[128,128]{1,0:T(8,128)S(1)} %cholesky.584), custom_call_target="Cholesky" | custom-call | tf_op jit(solution)/shard_map/jit(cholesky)/cholesky | solution.py:103
  310.6 9.8 %custom-call.64 = f32[1,128,128]{1,2,0:T(8,128)S(1)} custom-call(f32[1,128,128]{2,1,0:T(8,128)S(1)} %get-tuple-element.149), custom_call_target="InvertDiagBlocksLowerTriangular" | custom-call | tf_op jit(solution)/shard_map/jit(cholesky)/cholesky | solution.py:103
  323.8 11.7 %cholesky.468 = f32[128,128]{1,0:T(8,128)S(1)} custom-call(f32[128,128]{1,0:T(8,128)S(1)} %cholesky.589), custom_call_target="Cholesky" | custom-call | tf_op jit(solution)/shard_map/jit(cholesky)/cholesky | solution.py:103
  336.8 9.8 %custom-call.65 = f32[1,128,128]{1,2,0:T(8,128)S(1)} custom-call(f32[1,128,128]{2,1,0:T(8,128)S(1)} %get-tuple-element.146), custom_call_target="InvertDiagBlocksLowerTriangular" | custom-call | tf_op jit(solution)/shard_map/jit(cholesky)/cholesky | solution.py:103
  350.2 11.9 %cholesky.487 = f32[128,128]{1,0:T(8,128)S(1)} custom-call(f32[128,128]{1,0:T(8,128)S(1)} %cholesky.594), custom_call_target="Cholesky" | custom-call | tf_op jit(solution)/shard_map/jit(cholesky)/cholesky | solution.py:103
  363.4 9.8 %custom-call.66 = f32[1,128,128]{1,2,0:T(8,128)S(1)} custom-call(f32[1,128,128]{2,1,0:T(8,128)S(1)} %get-tuple-element.143), custom_call_target="InvertDiagBlocksLowerTriangular" | custom-call | tf_op jit(solution)/shard_map/jit(cholesky)/cholesky | solution.py:103
  376.7 11.7 %cholesky.506 = f32[128,128]{1,0:T(8,128)S(1)} custom-call(f32[128,128]{1,0:T(8,128)S(1)} %cholesky.599), custom_call_target="Cholesky" | custom-call | tf_op jit(solution)/shard_map/jit(cholesky)/cholesky | solution.py:103
  389.7 10.2 %custom-call.67 = f32[1,128,128]{1,2,0:T(8,128)S(1)} custom-call(f32[1,128,128]{2,1,0:T(8,128)S(1)} %get-tuple-element.140), custom_call_target="InvertDiagBlocksLowerTriangular" | custom-call | tf_op jit(solution)/shard_map/jit(cholesky)/cholesky | solution.py:103
  403.2 11.7 %cholesky.526 = f32[128,128]{1,0:T(8,128)S(1)} custom-call(f32[128,128]{1,0:T(8,128)S(1)} %cholesky.604), custom_call_target="Cholesky" | custom-call | tf_op jit(solution)/shard_map/jit(cholesky)/cholesky | solution.py:103
  416.2 9.8 %custom-call.68 = f32[1,128,128]{1,2,0:T(8,128)S(1)} custom-call(f32[1,128,128]{2,1,0:T(8,128)S(1)} %get-tuple-element.137), custom_call_target="InvertDiagBlocksLowerTriangular" | custom-call | tf_op jit(solution)/shard_map/jit(cholesky)/cholesky | solution.py:103
  429.0 11.9 %cholesky.546 = f32[128,128]{1,0:T(8,128)S(1)} custom-call(f32[128,128]{1,0:T(8,128)S(1)} %cholesky.609), custom_call_target="Cholesky" | custom-call | tf_op jit(solution)/shard_map/jit(cholesky)/cholesky | solution.py:103
  442.2 9.8 %custom-call.69 = f32[1,128,128]{1,2,0:T(8,128)S(1)} custom-call(f32[1,128,128]{2,1,0:T(8,128)S(1)} %get-tuple-element.134), custom_call_target="InvertDiagBlocksLowerTriangular" | custom-call | tf_op jit(solution)/shard_map/jit(cholesky)/cholesky | solution.py:103
  454.7 11.7 %cholesky.564 = f32[128,128]{1,0:T(8,128)S(1)} custom-call(f32[128,128]{1,0:T(8,128)S(1)} %convolution_subtract_fusion.11), custom_call_target="Cholesky" | custom-call | tf_op jit(solution)/shard_map/jit(cholesky)/cholesky | solution.py:103
  472.7 6.8 fusion.7
  479.5 27.6 %while.31 = (s32[]{:T(128)}, f32[1024,1024]{1,0:T(8,128)}, s32[8,2]{0,1:T(2,128)S(1)}, f32[8,128,128]{2,1,0:T(8,128)}, s32[]{:T(128)}) while((s32[]{:T(128)}, f32[1024,1024]{1,0:T(8,128)}, s32[8,2]{0,1:T(2,128)S(1)}, f32[8,128,128]{2,1,0:T(8,128)}, s32[]{:T(128)}) %tuple.101), condition=%wide.while_cond, body=%wide.while_body.sunk | while | flops 2 | bytes 132205 | solution.py:104
  507.1 79.6 %custom-call.70 = f32[8,128,128]{1,2,0:T(8,128)S(1)} custom-call(f32[8,128,128]{2,1,0:T(8,128)} %get-tuple-element.55), custom_call_target="InvertDiagBlocksLowerTriangular" | custom-call | tf_op jit(solution)/shard_map/jit(_solve_triangular)/triangular_solve | solution.py:104
  619.5 61.2 %while.30 = (s32[]{:T(128)}, f32[256,1024]{1,0:T(8,128)S(1)}, f32[256]{0:T(256)S(1)}, f32[1024]{0:T(1024)S(1)}, s32[]{:T(128)}) while((s32[]{:T(128)}, f32[256,1024]{1,0:T(8,128)S(1)}, f32[256]{0:T(256)S(1)}, f32[1024]{0:T(1024)S(1)}, s32[]{:T(128)}) %tuple.113), condition=%wide.region_24.25_spmd, body=%wide.region_23.24_spmd.sunk | while | flops 3147010 | bytes 2112573 | solution.py:42
  685.7 6.9 fusion.31
  (205 shorter events, 279.5 us)
Async XLA Ops:
  7.2 81.4 %all-gather.4.cloned.1.call-start = ((), (), s32[]{:S(2)}) async-start(), calls=%async_computation | async-start | bytes 12681216 | tf_op jit(solution)/shard_map/all_gather | solution.py:84
  9.4 233.8 %all-gather.6.cloned.1.call-start = ((), (), s32[]{:S(2)}) async-start(), calls=%async_computation.1 | async-start | bytes 4227072 | tf_op jit(solution)/shard_map/all_gather | solution.py:98
  11.3 87.9 %copy-start.5 = (f32[256]{0:T(256)}, f32[256]{0:T(256)S(1)}, u32[]{:S(2)}) copy-start(f32[256]{0:T(256)S(1)} %multiply_add_fusion.4) | copy-start | bytes 3076
  99.2 10.8 %copy-start.4 = (bf16[256,3072]{1,0:T(8,128)(2,1)S(1)}, bf16[256,3072]{1,0:T(8,128)(2,1)}, u32[]{:S(2)}) copy-start(bf16[256,3072]{1,0:T(8,128)(2,1)} %param.7) | copy-start | bytes 4718596
  105.7 4.6 copy-start
  110.3 4.5 copy-start.7
  176.7 504.0 %all-gather.8.cloned.1.call-start = ((), (), s32[]{:S(2)}) async-start(), calls=%async_computation.2 | async-start | bytes 4227072 | tf_op jit(solution)/shard_map/all_gather | solution.py:120
  258.1 2.1 copy-start.2
  586.7 3.9 copy-start.1
  614.5 71.2 %copy-start.3 = (f32[256,1024]{1,0:T(8,128)}, f32[256,1024]{1,0:T(8,128)S(1)}, u32[]{:S(2)}) copy-start(f32[256,1024]{1,0:T(8,128)S(1)} %convolution_select_fusion) | copy-start | bytes 3145732
  614.5 4.9 copy-start.6
Sparse Core Ops, SparseCore 0:
  11.6 76.9 all-gather.3
  176.8 66.3 all-gather.5
  615.4 64.3 all-gather.7
where the time goes:
time: 708 us; the launch traced here: 700 us
  other arithmetic  412 us (58%)
  waiting for transfers between devices  121 us (17%)
  local copies, waits for them, and re-layouts  78.8 us (11%)
  matrix products  64.6 us (9%)
  between operations  22.5 us (3%)
    another operation x31, other arithmetic, body(): lower = jnp.linalg.cholesky(diagonal_block)  182 us
    add x20, other arithmetic, one_layer(): weight_var / (2.0 * math.pi) * scales  121 us
    another operation x3, other arithmetic, body(): jax.scipy.linalg.solve_triangular(lower, identity, lower=True)  86.4 us
    all_gather x1, waiting for transfers between devices, body(): gathered = lax.all_gather(own_rows, ('row', 'sub'), axis=0, tiled=True)  74.1 us
    all_gather x1, waiting for transfers between devices, body(): lax.all_gather(outgoing, ('row', 'sub'), axis=0, tiled=True)  46.9 us
    another operation x25, local copies, waits for them, and re-layouts  27.7 us
    another operation x14, matrix products, body(): lower = jnp.linalg.cholesky(diagonal_block)  23.1 us
    gather x4, local copies, waits for them, and re-layouts, reorder(): return blocks[sources].reshape(PANEL, -1)  22.9 us
  transfers between devices with their start and end apart: 3, of which 2 were waited for; matrix products, arithmetic and copies ran while one was open for 12% of the time, Pallas kernels for 0%

commit v1 on v0

v1 whole, which is shorter than its diff:
```python
import math

import jax
import jax.numpy as jnp
from jax import lax
from jax.experimental import pallas as pl
from jax.experimental.pallas import tpu as pltpu
from jax.sharding import PartitionSpec as P

PANEL = 1024
DEPTH = 10
GROUP = 8
TILE = 128
STEPS = PANEL // TILE

weight_var = 2.0
bias_var = 0.1
noise_var = 0.1
f32 = jnp.float32
bf16 = jnp.bfloat16

ARC = (
    0.30010470747947693,
    0.015018727630376816,
    0.0023307923693209887,
    0.0007760883891023695,
    -0.00012745900312438607,
    0.00020702359324786812,
)


def nn(a, b):
    return lax.dot_general(a, b, (((1,), (0,)), ((), ())), preferred_element_type=f32)


def nt(a, b):
    return lax.dot_general(a, b, (((1,), (1,)), ((), ())), preferred_element_type=f32)


def split3(x):
    h = x.astype(bf16)
    r = x - h.astype(f32)
    m = r.astype(bf16)
    l = (r - m.astype(f32)).astype(bf16)
    return h, m, l


def lhs6(x):
    h, m, l = split3(x)
    return jnp.concatenate([h, m, h, m, h, l], 1)


def rhs6_nn(x):
    h, m, l = split3(x)
    return jnp.concatenate([h, h, m, m, l, h], 0)


def rhs6_nt(x):
    h, m, l = split3(x)
    return jnp.concatenate([h, h, m, m, l, h], 1)


def own_square(rows_ref, start):
    rows = rows_ref[start : start + TILE, :]
    gram = nt(rows, rows)
    eye = lax.broadcasted_iota(jnp.int32, (TILE, TILE), 0) == lax.broadcasted_iota(
        jnp.int32, (TILE, TILE), 1
    )
    only = jnp.where(eye, gram, 0.0)
    scale = weight_var / rows_ref.shape[1]
    return (
        jnp.sum(only, axis=0, keepdims=True) * scale + bias_var,
        jnp.sum(only, axis=1, keepdims=True) * scale + bias_var,
    )


def layer_scales(q):
    inv = [lax.rsqrt(q + bias_var * n) for n in range(DEPTH)]
    ratio = [(q + bias_var * n) * inv[n] * inv[n + 1] for n in range(DEPTH - 1)]
    offset = [inv[n + 1] * math.sqrt(bias_var) for n in range(DEPTH - 1)]
    last = (q + bias_var * (DEPTH - 1)) * inv[DEPTH - 1]
    return inv[0], ratio, offset, last


def store_columns(tab_ref, start, q):
    first, ratio, offset, last = layer_scales(q)
    for at, row in enumerate([first] + ratio + offset + [last]):
        tab_ref[at : at + 1, start : start + TILE] = row


def relu_layers(gram, q_rows, tab_ref, lo, width):
    first, ratio, offset, last = layer_scales(q_rows)
    pieces = width // TILE
    col = lambda at, w: jnp.broadcast_to(
        tab_ref[at : at + 1, lo + w * TILE : lo + (w + 1) * TILE], (GROUP, TILE)
    )
    scale = weight_var / 3072
    c = [
        (gram[:, w * TILE : (w + 1) * TILE] * scale + bias_var) * (first * col(0, w))
        for w in range(pieces)
    ]
    for n in range(DEPTH):
        for w in range(pieces):
            u = jnp.maximum(1.0 - jnp.abs(c[w]), 1e-30)
            p = ARC[5] * u + ARC[4]
            for k in (3, 2, 1, 0):
                p = p * u + ARC[k]
            g = jnp.maximum(c[w], 0.0) + (u * u) * lax.rsqrt(u) * p
            if n < DEPTH - 1:
                c[w] = g * (ratio[n] * col(1 + n, w)) + offset[n] * col(DEPTH + n, w)
            else:
                c[w] = g * (last * col(2 * DEPTH - 1, w)) + bias_var
    return jnp.concatenate(c, axis=1)


def block_inverse(d_ref):
    lane = lax.broadcasted_iota(jnp.int32, (8, TILE), 1)
    sub = lax.broadcasted_iota(jnp.int32, (8, TILE), 0)
    spread = lambda x: jnp.broadcast_to(x, (8, TILE))
    for s in range(TILE // 8):
        r0 = 8 * s
        inside = (lane >= r0) & (lane < r0 + 8)
        rows = [spread(d_ref[r0 + j : r0 + j + 1, :]) for j in range(8)]
        e = [
            [spread(rows[i][:, r0 + j : r0 + j + 1]) if j >= i else None for j in range(8)]
            for i in range(8)
        ]
        below = {}
        for i in range(s + 1, TILE // 8):
            b = d_ref[8 * i : 8 * i + 8, :]
            below[i] = (b, [spread(b[:, r0 + j : r0 + j + 1]) for j in range(8)])
        u = [jnp.where(inside, (lane == r0 + j).astype(f32), rows[j]) for j in range(8)]
        ys, rs = [], []
        for j in range(8):
            y = lax.rsqrt(e[j][j])
            r = y * y
            ys.append(y)
            rs.append(r)
            for i in range(j + 1, 8):
                f = e[j][i] * r
                for q in range(i, 8):
                    e[i][q] = e[i][q] - f * e[j][q]
                u[i] = u[i] - f * u[j]
        out = u[7] * ys[7]
        for j in range(6, -1, -1):
            out = jnp.where(sub == j, u[j] * ys[j], out)
        g = [None] * 8
        for j in range(7, -1, -1):
            acc = u[j] * rs[j]
            for i in range(j + 1, 8):
                acc = acc - (e[j][i] * rs[j]) * g[i]
            g[j] = acc
        d_ref[r0 : r0 + 8, :] = out
        for i in range(s + 1, TILE // 8):
            b, c = below[i]
            acc = jnp.where(inside, 0.0, b)
            for j in range(8):
                acc = acc - c[j] * g[j]
            d_ref[8 * i : 8 * i + 8, :] = acc


def place_points(src_ref, raw_ref, p_ref):
    def place(b, carry):
        pair = [raw_ref[src_ref[2 * b + n]].astype(f32) for n in range(2)]
        at = pl.ds(pl.multiple_of(b * 2 * GROUP, 2 * GROUP), 2 * GROUP)
        p_ref[at, :] = jnp.concatenate(pair, axis=0).astype(bf16)
        return carry

    lax.fori_loop(0, PANEL // (2 * GROUP), place, 0)


def local_kernel(info_ref, x_ref, q_ref, p_ref, out_ref, tab_ref, after):
    for b in range(PANEL // 256):
        out_ref[:, b * 256 : (b + 1) * 256] = nt(x_ref[...], p_ref[b * 256 : (b + 1) * 256, :])
    start = info_ref[0] + after
    place = info_ref[1 + after] * GROUP
    column = lax.broadcasted_iota(jnp.int32, (GROUP, PANEL), 1)
    within = lax.broadcasted_iota(jnp.int32, (GROUP, PANEL), 0)

    def clear(r, carry):
        at = pl.ds(pl.multiple_of(r * GROUP, GROUP), GROUP)
        out_ref[at, :] = jnp.zeros((GROUP, PANEL), f32)
        return carry

    lax.fori_loop(0, start, clear, 0)

    def row_block(r, carry):
        at = pl.ds(pl.multiple_of(r * GROUP, GROUP), GROUP)
        k = relu_layers(out_ref[at, :], q_ref[at, :], tab_ref, 0, PANEL)
        own = (r == start) & (column == place + within)
        out_ref[at, :] = k + jnp.where(own, noise_var, 0.0)
        return carry

    lax.fori_loop(start, out_ref.shape[0] // GROUP, row_block, 0)


def panel_kernel(info_ref, src_ref, x_ref, q_ref, raw_ref, out_ref, a_ref, p_ref, tab_ref, qrow_ref):
    place_points(src_ref, raw_ref, p_ref)
    for b in range(STEPS):
        along, down = own_square(p_ref, b * TILE)
        store_columns(tab_ref, b * TILE, along)
        qrow_ref[b * TILE : (b + 1) * TILE, :] = jnp.broadcast_to(down, (TILE, TILE))
    local_kernel(info_ref, x_ref, q_ref, p_ref, out_ref, tab_ref, 0)
    for b in range(PANEL // 256):
        lo = b * 256
        for c in range(b, PANEL // 256):
            a_ref[lo : lo + 256, c * 256 : (c + 1) * 256] = nt(
                p_ref[lo : lo + 256, :], p_ref[c * 256 : (c + 1) * 256, :]
            )

        def row_block(r, carry, lo=lo):
            at = pl.ds(pl.multiple_of(r * GROUP, GROUP), GROUP)
            width = PANEL - lo
            k = relu_layers(a_ref[at, lo:], qrow_ref[at, :], tab_ref, lo, width)
            column = lax.broadcasted_iota(jnp.int32, (GROUP, width), 1) + lo
            within = lax.broadcasted_iota(jnp.int32, (GROUP, width), 0)
            a_ref[at, lo:] = k + jnp.where(column == r * GROUP + within, noise_var, 0.0)
            return carry

        lax.fori_loop(lo // GROUP, (lo + 256) // GROUP, row_block, 0)


def next_kernel(info_ref, src_ref, x_ref, q_ref, raw_ref, out_ref, p_ref, tab_ref):
    place_points(src_ref, raw_ref, p_ref)
    for b in range(STEPS):
        store_columns(tab_ref, b * TILE, own_square(p_ref, b * TILE)[0])
    local_kernel(info_ref, x_ref, q_ref, p_ref, out_ref, tab_ref, 1)


def factor_kernel(info_ref, k_ref, m_ref, f_ref, a_ref, inv_ref, d_ref):
    a_ref[...] = m_ref[...]
    row = lax.broadcasted_iota(jnp.int32, (TILE, TILE), 0)
    col = lax.broadcasted_iota(jnp.int32, (TILE, TILE), 1)
    f_ref[...] = k_ref[...]

    def step(k, carry):
        k0 = pl.multiple_of(k * TILE, TILE)
        d_ref[...] = a_ref[pl.ds(k0, TILE), pl.ds(k0, TILE)]
        block_inverse(d_ref)
        linv = jnp.where(row >= col, d_ref[...], 0.0)
        inv_ref[k] = linv
        for kk in range(STEPS - 1):

            @pl.when(k == kk)
            def _():
                b0, c0 = kk * TILE, (kk + 1) * TILE
                u = nn(lhs6(linv), rhs6_nn(a_ref[b0:c0, c0:]))
                a_ref[b0:c0, c0:] = u
                u6 = rhs6_nn(u)
                for i in range(kk + 1, STEPS):
                    i0 = i * TILE
                    x = u[:, i0 - c0 : i0 - c0 + TILE].T
                    a_ref[i0 : i0 + TILE, i0:] = a_ref[i0 : i0 + TILE, i0:] - nn(
                        lhs6(x), u6[:, i0 - c0 :]
                    )

        return carry

    lax.fori_loop(0, STEPS, step, 0)

    for k in range(STEPS):
        b0, c0 = k * TILE, (k + 1) * TILE
        x = nt(lhs6(f_ref[:, b0:c0]), rhs6_nt(inv_ref[k]))
        f_ref[:, b0:c0] = x
        if k < STEPS - 1:
            f_ref[:, c0:] = f_ref[:, c0:] - nn(lhs6(x), rhs6_nn(a_ref[b0:c0, c0:]))

    at = pl.ds(pl.multiple_of(info_ref[0] * GROUP, GROUP), GROUP)
    column = lax.broadcasted_iota(jnp.int32, (GROUP, PANEL), 1)
    within = lax.broadcasted_iota(jnp.int32, (GROUP, PANEL), 0)
    f_ref[at, :] = jnp.where(column <= info_ref[1] * GROUP + within, f_ref[at, :], 0.0)


def update_kernel(info_ref, src_ref, f_ref, a_ref, inv_ref, nk_ref, nl_ref, out_ref, g_ref, kn_ref):
    def place(b, carry):
        at = pl.ds(pl.multiple_of(b * GROUP, GROUP), GROUP)
        kn_ref[at, :] = nk_ref[src_ref[b]]
        return carry

    lax.fori_loop(0, PANEL // GROUP, place, 0, unroll=8)
    for k in range(STEPS - 1, -1, -1):
        b0, c0 = k * TILE, (k + 1) * TILE
        x = f_ref[:, b0:c0]
        for j in range(k + 1, STEPS):
            j0 = j * TILE
            x = x - nt(lhs6(g_ref[:, j0 : j0 + TILE]), rhs6_nt(a_ref[b0:c0, j0 : j0 + TILE]))
        g_ref[:, b0:c0] = nn(lhs6(x), rhs6_nn(inv_ref[k]))
    rows = lax.broadcasted_iota(jnp.int32, (f_ref.shape[0], 256), 0) // GROUP
    live = rows > info_ref[0]
    for b in range(PANEL // 256):
        total = nl_ref[:, b * 256 : (b + 1) * 256]
        for k in range(STEPS):
            k0 = k * TILE
            total = total - nt(
                lhs6(g_ref[:, k0 : k0 + TILE]),
                rhs6_nt(kn_ref[b * 256 : (b + 1) * 256, k0 : k0 + TILE]),
            )
        out_ref[:, b * 256 : (b + 1) * 256] = jnp.where(live, total, 0.0)


SMEM = pl.BlockSpec(memory_space=pltpu.SMEM)
VMEM = pl.BlockSpec(memory_space=pltpu.VMEM)
PARAMS = pltpu.CompilerParams(vmem_limit_bytes=56 * 1024 * 1024)


def row_variance(rows):
    values = rows.astype(f32)
    return jnp.sum(values * values, axis=1) * (weight_var / rows.shape[1]) + bias_var


def body(images, block_id, panel_index):
    rows_dev, features = images.shape
    shards = lax.axis_size("row") * lax.axis_size("sub")
    myself = lax.axis_index("row") * lax.axis_size("sub") + lax.axis_index("sub")
    panel = panel_index[0]
    everyone = jnp.arange(shards, dtype=jnp.int32)
    local_var = jnp.broadcast_to(row_variance(images)[:, None], (rows_dev, TILE))

    def arrangement(which):
        positions = lax.dynamic_index_in_dim(block_id, which, 1, keepdims=False) - which * shards
        sources = jnp.sum(
            jnp.where(positions[None, :] == everyone[:, None], everyone[None, :], 0), axis=1
        )
        return sources, positions[myself]

    def gather(block):
        return lax.all_gather(block, ("row", "sub"), axis=0, tiled=True).reshape(
            shards, GROUP, -1
        )

    def own(which, array):
        return lax.dynamic_slice_in_dim(array, which * GROUP, GROUP, 0)

    sources, position = arrangement(panel)
    next_sources, next_position = arrangement(panel + 1)
    info = jnp.stack([panel, position, next_position])
    points = gather(own(panel, images))
    next_points = gather(own(panel + 1, images))
    table = pltpu.VMEM((24, PANEL), f32)
    placed = pltpu.VMEM((PANEL, features), bf16)
    rows_out = jax.ShapeDtypeStruct((rows_dev, PANEL), f32)
    square = jax.ShapeDtypeStruct((PANEL, PANEL), f32)

    matrix, diagonal = pl.pallas_call(
        panel_kernel,
        out_shape=(rows_out, square),
        in_specs=[SMEM, SMEM, VMEM, VMEM, VMEM],
        out_specs=(VMEM, VMEM),
        scratch_shapes=[placed, table, pltpu.VMEM((PANEL, TILE), f32)],
        compiler_params=PARAMS,
        name="panel_kernel",
        cost_estimate=pl.CostEstimate(flops=3 * 10**10, bytes_accessed=16 << 20, transcendentals=0),
    )(info, sources, images, local_var, points)
    next_rows = gather(own(panel + 1, matrix))
    factor, upper, inverses = pl.pallas_call(
        factor_kernel,
        out_shape=(rows_out, square, jax.ShapeDtypeStruct((STEPS, TILE, TILE), f32)),
        in_specs=[SMEM, VMEM, VMEM],
        out_specs=(VMEM, VMEM, VMEM),
        scratch_shapes=[pltpu.VMEM((TILE, TILE), f32)],
        compiler_params=PARAMS,
        name="factor_kernel",
        cost_estimate=pl.CostEstimate(flops=10**11, bytes_accessed=16 << 20, transcendentals=0),
    )(info, matrix, diagonal)
    next_matrix = pl.pallas_call(
        next_kernel,
        out_shape=rows_out,
        in_specs=[SMEM, SMEM, VMEM, VMEM, VMEM],
        out_specs=VMEM,
        scratch_shapes=[placed, table],
        compiler_params=PARAMS,
        name="next_kernel",
        cost_estimate=pl.CostEstimate(flops=2 * 10**10, bytes_accessed=16 << 20, transcendentals=0),
    )(info, next_sources, images, local_var, next_points)
    updated = pl.pallas_call(
        update_kernel,
        out_shape=jax.ShapeDtypeStruct((rows_dev, PANEL), f32),
        in_specs=[SMEM, SMEM, VMEM, VMEM, VMEM, VMEM, VMEM],
        out_specs=VMEM,
        scratch_shapes=[pltpu.VMEM((rows_dev, PANEL), f32), pltpu.VMEM((PANEL, PANEL), f32)],
        compiler_params=PARAMS,
        name="update_kernel",
        cost_estimate=pl.CostEstimate(flops=10**10, bytes_accessed=16 << 20, transcendentals=0),
    )(info, next_sources, factor, upper, inverses, next_rows, next_matrix)
    return (factor, updated)


def solution(mesh):
    in_specs = (P(("row", "sub"), None), P(), P())
    out_specs = (P(("row", "sub"), None), P(("row", "sub"), None))
    return jax.shard_map(body, mesh=mesh, in_specs=in_specs, out_specs=out_specs, check_vma=False)
```

time: 708 us -> 245 us (0.35); the launches traced: 700 us -> 244 us
  other arithmetic: 412 us -> 5.67 us
  Pallas kernels: 0 us -> 137 us
  local copies, waits for them, and re-layouts: 78.8 us -> 4.24 us
  matrix products: 64.6 us -> 0 us
  waiting for transfers between devices: 121 us -> 83.2 us
  between operations: 22.5 us -> 14.4 us
    another operation x34 -> x1, other arithmetic: 268 us -> 1.78 us  [body(): info = jnp.stack([panel, position, next_position])]
    pallas_call x0 -> x4, Pallas kernels: none -> 137 us  [the longest x1 59.3 us: body(): pl.pallas_call(factor_kernel, out_shape=(rows_out, square, jax.ShapeDtype...]
    add x63 -> x0, other arithmetic: 123 us -> none  [the longest x20 121 us: one_layer(): weight_var / (2.0 * math.pi) * scales]
    another operation x29 -> x0, matrix products: 46 us -> none  [the longest x14 23.1 us: body(): lower = jnp.linalg.cholesky(diagonal_block)]
    all_gather x3, waiting for transfers between devices: 121 us -> 82.5 us  [gather(): lax.all_gather(block, ('row', 'sub'), axis=0, tiled=True)]
    another operation x34 -> x0, local copies, waits for them, and re-layouts: 30.3 us -> none
    gather x4 -> x0, local copies, waits for them, and re-layouts: 22.9 us -> none  [reorder(): return blocks[sources].reshape(PANEL, -1)]
    dot_general x4 -> x0, matrix products: 18.6 us -> none  [the longest x2 10.7 us: product_nt(): lax.dot_general(left, right, (((1,), (1,)), ((), ())), precision=lax.Prec...]
  transfers between devices with their start and end apart: 3 -> 3, of which waited for: 2 -> 2; matrix products, arithmetic and copies ran while one was open for 12% -> 3% of each run, Pallas kernels for 0% -> 50%
where the time goes in v1:
time: 245 us; the launch traced here: 244 us
  Pallas kernels  137 us (56%)
  waiting for transfers between devices  83.2 us (34%)
  between operations  14.4 us (6%)
  other arithmetic  5.67 us (2%)
  local copies, waits for them, and re-layouts  4.24 us (2%)
    all_gather x3, waiting for transfers between devices, gather(): lax.all_gather(block, ('row', 'sub'), axis=0, tiled=True)  82.5 us
    pallas_call x1, Pallas kernels, body(): pl.pallas_call(factor_kernel, out_shape=(rows_out, square, jax.ShapeDtype...  59.3 us
    pallas_call x1, Pallas kernels, body(): pl.pallas_call(panel_kernel, out_shape=(rows_out, square), in_specs=[SMEM...  51.1 us
    pallas_call x1, Pallas kernels, body(): pl.pallas_call(update_kernel, out_shape=jax.ShapeDtypeStruct((rows_dev, P...  14.8 us
    pallas_call x1, Pallas kernels, body(): pl.pallas_call(next_kernel, out_shape=rows_out, in_specs=[SMEM, SMEM, VME...  11.5 us
  transfers between devices with their start and end apart: 3, of which 2 were waited for; matrix products, arithmetic and copies ran while one was open for 3% of the time, Pallas kernels for 50%

profile of v1, /device:TPU:1, one launch (start us, length us, event | category | flops | bytes accessed | tf_op | source)
XLA Modules:
  0.0 244.5 jit_solution(12841556861390471602)
XLA Ops:
  7.2 0.0 all-gather.4.cloned.1.call-start
  7.9 1.5 constant_dynamic-slice_fusion
  9.3 0.0 all-gather.4.cloned.1.call-update
  9.4 0.0 all-gather.8.cloned.1.call-start
  9.4 0.7 all-gather.8.cloned.1.call-update
  10.1 0.0 all-gather.6.cloned.1.call-start
  10.2 0.8 fusion
  11.0 0.7 constant_dynamic-slice_fusion.3
  11.6 1.8 pad_add_fusion.info_ref
  13.4 0.6 select_reduce_fusion.src_ref
  14.0 0.7 select_reduce_fusion.1.src_ref
  14.7 1.8 multiply_reduce_fusion
  16.5 66.9 %all-gather.4.cloned.1.call-done = bf16[1024,3072]{1,0:T(8,128)(2,1)} async-done(((bf16[8,3072]{1,0:T(8,128)(2,1)}), bf16[1024,3072]{1,0:T(8,128)(2,1)}) %all-gather.4.cloned.1.call-update) | async-done | bytes 6291472 | tf_op jit(solution)/shard_map/all_gather | solution.py:327
  83.4 0.8 broadcast_in_dim.32.q_ref
  84.2 51.1 %panel_kernel.1 = (f32[256,1024]{1,0:T(8,128)}, f32[1024,1024]{1,0:T(8,128)}) custom-call(s32[3]{0:T(128)} %pad_add_fusion.info_ref, s32[128]{0:T(128)} %select_reduce_fusion.1.src_ref, bf16[256,3072]{1,0:T(8,128)(2,1)} %x_ref.3, f32[256,128]{1,0:T(8,128)} %broadcast_in_dim.32.q_ref, bf16[128,8,3072]{2,1,0:T(8,128)(2,1)} %bitcast.18), custom_call_target="tpu_custom_call" | custom-call | flops 30000001024 | bytes 16777216 | tf_op jit(solution)/shard_map/panel_kernel/pallas_call | solution.py:344
  135.3 1.4 constant_dynamic-slice_fusion.1
  136.7 0.0 all-gather.6.cloned.1.call-update
  136.7 15.6 %all-gather.8.cloned.1.call-done = bf16[1024,3072]{1,0:T(8,128)(2,1)} async-done(((bf16[8,3072]{1,0:T(8,128)(2,1)}), bf16[1024,3072]{1,0:T(8,128)(2,1)}) %all-gather.8.cloned.1.call-update) | async-done | bytes 6291472 | tf_op jit(solution)/shard_map/all_gather | solution.py:327
  152.3 11.5 %next_kernel.1.nl_ref = f32[256,1024]{1,0:T(8,128)} custom-call(s32[3]{0:T(128)} %pad_add_fusion.info_ref, s32[128]{0:T(128)} %select_reduce_fusion.src_ref, bf16[256,3072]{1,0:T(8,128)(2,1)} %x_ref.3, f32[256,128]{1,0:T(8,128)} %broadcast_in_dim.32.q_ref, bf16[128,8,3072]{2,1,0:T(8,128)(2,1)} %bitcast.17), custom_call_target="tpu_custom_call" | custom-call | flops 20000000000 | bytes 16777216 | tf_op jit(solution)/shard_map/next_kernel/pallas_call | solution.py:365
  163.8 59.3 %factor_kernel.1 = (f32[256,1024]{1,0:T(8,128)}, f32[1024,1024]{1,0:T(8,128)}, f32[8,128,128]{2,1,0:T(8,128)}) custom-call(s32[3]{0:T(128)} %pad_add_fusion.info_ref, f32[256,1024]{1,0:T(8,128)} %get-tuple-element.7.k_ref, f32[1024,1024]{1,0:T(8,128)} %get-tuple-element.8.m_ref), custom_call_target="tpu_custom_call" | custom-call | flops 99999997952 | bytes 16777216 | tf_op jit(solution)/shard_map/factor_kernel/pallas_call | solution.py:355
  223.1 0.0 all-gather.6.cloned.1.call-done
  223.1 14.8 %update_kernel.1 = f32[256,1024]{1,0:T(8,128)} custom-call(s32[3]{0:T(128)} %pad_add_fusion.info_ref, s32[128]{0:T(128)} %select_reduce_fusion.src_ref, f32[256,1024]{1,0:T(8,128)} %get-tuple-element.5.f_ref, f32[1024,1024]{1,0:T(8,128)} %get-tuple-element.10.a_ref, f32[8,128,128]{2,1,0:T(8,128)} %get-tuple-element.11.inv_ref, f32[128,8,1024]{2,1,0:T(8,128)} %bitcast.19, ...), custom_call_target="tpu_custom_call" | custom-call | flops 10000000000 | bytes 16777216 | tf_op jit(solution)/shard_map/update_kernel/pallas_call | solution.py:375
  (1 shorter events, 0.0 us)
Async XLA Ops:
  7.2 76.3 %all-gather.4.cloned.1.call-start = ((), (), s32[]{:S(2)}) async-start(), calls=%async_computation | async-start | bytes 6340608 | tf_op jit(solution)/shard_map/all_gather | solution.py:327
  9.4 142.9 %all-gather.8.cloned.1.call-start = ((), (), s32[]{:S(2)}) async-start(), calls=%async_computation.2 | async-start | bytes 6340608 | tf_op jit(solution)/shard_map/all_gather | solution.py:327
  10.1 213.0 %all-gather.6.cloned.1.call-start = ((), (), s32[]{:S(2)}) async-start(), calls=%async_computation.1 | async-start | bytes 4227072 | tf_op jit(solution)/shard_map/all_gather | solution.py:327
Sparse Core Ops, SparseCore 0:
  11.6 71.8 all-gather.3
  86.4 65.8 all-gather.7
  155.4 64.5 all-gather.5

commit v2 on v1

--- a/solution.py
+++ b/solution.py
@@ -298,6 +298,123 @@
         out_ref[:, b * 256 : (b + 1) * 256] = jnp.where(live, total, 0.0)
 
 
+ORDERS = (("x", "y", "z"), ("y", "z", "x"), ("z", "x", "y"))
+
+
+def gather_kernel(block_ref, out_ref, near_send, near_recv, pair_send, pair_recv, own_sem, *, cuts):
+    row, sub = lax.axis_index("row"), lax.axis_index("sub")
+    me = {"z": row // 8, "y": row // 2 % 4, "x": sub}
+    core = row % 2
+
+    def device(at, core_at):
+        return (at["z"] * 8 + at["y"] * 2 + core_at, at["x"])
+
+    def shifted(axis, by):
+        return {**me, axis: (me[axis] + by + 4) % 4}
+
+    partner = device(me, 1 - core)
+    peers = [device(shifted(a, by), core) for a in "zyx" for by in (1, -1)] + [partner]
+    barrier = pltpu.get_barrier_semaphore()
+    for peer in peers:
+        pl.semaphore_signal(barrier, inc=1, device_id=peer, device_id_type=pl.DeviceIdType.MESH)
+    pl.semaphore_wait(barrier, len(peers))
+
+    def part(at, core_at, lo, hi):
+        return out_ref.at[at["z"], at["y"], core_at, at["x"], :, lo:hi]
+
+    def copy(src, dst, send, recv, to):
+        return pltpu.make_async_remote_copy(
+            src_ref=src,
+            dst_ref=dst,
+            send_sem=send,
+            recv_sem=recv,
+            device_id=to,
+            device_id_type=pl.DeviceIdType.MESH,
+        )
+
+    every = pl.ds(0, 4)
+    width = block_ref.shape[1]
+    mine = pltpu.make_async_copy(block_ref, part(me, core, 0, width), own_sem)
+    mine.start()
+    sent = []
+
+    def to_partner(at, lo, hi, slot):
+        c = copy(part(at, core, lo, hi), part(at, core, lo, hi), pair_send.at[slot], pair_recv.at[slot], partner)
+        c.start()
+        arriving.append(
+            copy(part(at, 1 - core, lo, hi), part(at, 1 - core, lo, hi), pair_send.at[slot], pair_recv.at[slot], partner)
+        )
+        sent.append(c)
+
+    arriving = []
+    for t in range(3):
+        held = []
+        for s, order in enumerate(ORDERS):
+            lo, mid, hi = cuts[s]
+            axis = order[t]
+            sets = {
+                by: {**{a: every if order.index(a) < t else me[a] for a in "zyx"}, axis: (me[axis] + by + 4) % 4}
+                for by in (0, 1, -1, 2)
+            }
+            up, down = device(shifted(axis, 1), core), device(shifted(axis, -1), core)
+
+            def near(kind, by, a, b, to, s=s, t=t, sets=sets):
+                piece = part(sets[by], core, a, b)
+                source = block_ref.at[:, a:b] if t == 0 and by == 0 else piece
+                return copy(source, piece, near_send.at[s, t, kind], near_recv.at[s, t, kind], to)
+
+            for kind, to in ((0, up), (1, down)):
+                c = near(kind, 0, lo, hi, to)
+                c.start()
+                sent.append(c)
+            held.append((near, sets, up, down, lo, mid, hi))
+        if t == 0:
+            mine.wait()
+            to_partner(me, 0, width, 27)
+        for s, (near, sets, up, down, lo, mid, hi) in enumerate(held):
+            near(0, -1, lo, hi, up).wait_recv()
+            c = near(2, -1, lo, mid, up)
+            c.start()
+            sent.append(c)
+            near(1, 1, lo, hi, down).wait_recv()
+            c = near(3, 1, mid, hi, down)
+            c.start()
+            sent.append(c)
+            to_partner(sets[-1], lo, hi, 9 * s + 3 * t)
+            to_partner(sets[1], lo, hi, 9 * s + 3 * t + 1)
+        for s, (near, sets, up, down, lo, mid, hi) in enumerate(held):
+            near(2, 2, lo, mid, up).wait_recv()
+            near(3, 2, mid, hi, down).wait_recv()
+            to_partner(sets[2], lo, hi, 9 * s + 3 * t + 2)
+    for c in arriving:
+        c.wait_recv()
+    for c in sent:
+        c.wait_send()
+
+
+def gather_blocks(block, collective_id):
+    rows, width = block.shape
+    tiles = width // 128
+    first = [0, tiles * 3 // 8 if tiles % 3 else tiles // 3, tiles * 3 // 4 if tiles % 3 else 2 * tiles // 3, tiles]
+    cuts = [(128 * a, 128 * ((a + b + 1) // 2), 128 * b) for a, b in zip(first, first[1:])]
+    out = pl.pallas_call(
+        lambda *refs: gather_kernel(*refs, cuts=cuts),
+        out_shape=jax.ShapeDtypeStruct((4, 4, 2, 4, rows, width), block.dtype),
+        in_specs=[pl.BlockSpec(memory_space=pl.ANY)],
+        out_specs=pl.BlockSpec(memory_space=pl.ANY),
+        scratch_shapes=[
+            pltpu.SemaphoreType.DMA((3, 3, 4)),
+            pltpu.SemaphoreType.DMA((3, 3, 4)),
+            pltpu.SemaphoreType.DMA((28,)),
+            pltpu.SemaphoreType.DMA((28,)),
+            pltpu.SemaphoreType.DMA,
+        ],
+        compiler_params=pltpu.CompilerParams(collective_id=collective_id, has_side_effects=True),
+        name="gather_kernel",
+    )(block)
+    return out.reshape(128, rows, width)
+
+
 SMEM = pl.BlockSpec(memory_space=pltpu.SMEM)
 VMEM = pl.BlockSpec(memory_space=pltpu.VMEM)
 PARAMS = pltpu.CompilerParams(vmem_limit_bytes=56 * 1024 * 1024)
@@ -334,7 +451,7 @@
     sources, position = arrangement(panel)
     next_sources, next_position = arrangement(panel + 1)
     info = jnp.stack([panel, position, next_position])
-    points = gather(own(panel, images))
+    points = gather_blocks(own(panel, images), 0)
     next_points = gather(own(panel + 1, images))
     table = pltpu.VMEM((24, PANEL), f32)
     placed = pltpu.VMEM((PANEL, features), bf16)

time: 245 us -> 217 us (0.89)
  waiting for transfers between devices: 83.2 us -> 0.04 us
  Pallas kernels: 137 us -> 193 us
    all_gather x3 -> x2, waiting for transfers between devices: 82.5 us -> 0.01 us  [gather(): lax.all_gather(block, ('row', 'sub'), axis=0, tiled=True)]
    pallas_call x0 -> x1, Pallas kernels: none -> 40 us  [gather_blocks(): pl.pallas_call(lambda *refs: gather_kernel(*refs, cuts=cuts), out_shape=j...]
    pallas_call x1, Pallas kernels: 51.1 us -> 59.5 us  [body(): pl.pallas_call(panel_kernel, out_shape=(rows_out, square), in_specs=[SMEM...]
    pallas_call x1, Pallas kernels: 11.5 us -> 19.6 us  [body(): pl.pallas_call(next_kernel, out_shape=rows_out, in_specs=[SMEM, SMEM, VME...]
  transfers between devices with their start and end apart: 3 -> 2, of which waited for: 2 -> 0; matrix products, arithmetic and copies ran while one was open for 3% -> 3% of each run, Pallas kernels for 50% -> 82%
where the time goes in v2:
time: 217 us
  Pallas kernels  193 us (89%)
  between operations  14.9 us (7%)
  other arithmetic  4.28 us (2%)
  local copies, waits for them, and re-layouts  4.18 us (2%)
    pallas_call x1, Pallas kernels, body(): pl.pallas_call(factor_kernel, out_shape=(rows_out, square, jax.ShapeDtype...  59.5 us
    pallas_call x1, Pallas kernels, body(): pl.pallas_call(panel_kernel, out_shape=(rows_out, square), in_specs=[SMEM...  59.5 us
    pallas_call x1, Pallas kernels, gather_blocks(): pl.pallas_call(lambda *refs: gather_kernel(*refs, cuts=cuts), out_shape=j...  40 us
    pallas_call x1, Pallas kernels, body(): pl.pallas_call(next_kernel, out_shape=rows_out, in_specs=[SMEM, SMEM, VME...  19.6 us
    pallas_call x1, Pallas kernels, body(): pl.pallas_call(update_kernel, out_shape=jax.ShapeDtypeStruct((rows_dev, P...  14.9 us
  transfers between devices with their start and end apart: 2, of which 0 were waited for; matrix products, arithmetic and copies ran while one was open for 3% of the time, Pallas kernels for 82%

profile of v2, /device:TPU:1, one launch (start us, length us, event | category | flops | bytes accessed | tf_op | source)
XLA Modules:
  0.0 216.9 jit_solution(6968676949256670247)
XLA Ops:
  7.2 0.0 copy-start
  7.2 0.0 all-gather.5.cloned.1.call-start
  8.0 1.5 constant_dynamic-slice_fusion
  9.5 0.0 all-gather.5.cloned.1.call-update
  9.5 0.0 all-gather.3.cloned.1.call-start
  9.5 40.0 %gather_kernel.1 = bf16[4,4,2,4,8,3072]{5,4,3,2,1,0:T(8,128)(2,1)} custom-call(bf16[8,3072]{1,0:T(8,128)(2,1)} %get-tuple-element.13.refs_0_), custom_call_target="tpu_custom_call" | custom-call | tf_op jit(solution)/shard_map/gather_kernel/pallas_call | solution.py:400
  49.5 0.8 fusion
  50.3 0.6 constant_dynamic-slice_fusion.3
  50.9 1.8 pad_add_fusion.info_ref
  52.7 0.6 select_reduce_fusion.1.src_ref
  53.4 0.0 copy-done
  53.4 0.4 multiply_reduce_fusion
  53.8 0.7 broadcast_in_dim.32.q_ref
  54.5 59.5 %panel_kernel.1 = (f32[256,1024]{1,0:T(8,128)}, f32[1024,1024]{1,0:T(8,128)}) custom-call(s32[3]{0:T(128)} %pad_add_fusion.info_ref, s32[128]{0:T(128)} %select_reduce_fusion.1.src_ref, bf16[256,3072]{1,0:T(8,128)(2,1)} %x_ref.3, f32[256,128]{1,0:T(8,128)} %broadcast_in_dim.32.q_ref, bf16[128,8,3072]{2,1,0:T(8,128)(2,1)} %bitcast.15), custom_call_target="tpu_custom_call" | custom-call | flops 30000001024 | bytes 16777216 | tf_op jit(solution)/shard_map/panel_kernel/pallas_call | solution.py:461
  114.0 1.4 constant_dynamic-slice_fusion.1
  115.4 0.0 all-gather.3.cloned.1.call-update
  115.4 0.6 select_reduce_fusion.src_ref
  116.1 59.5 %factor_kernel.1 = (f32[256,1024]{1,0:T(8,128)}, f32[1024,1024]{1,0:T(8,128)}, f32[8,128,128]{2,1,0:T(8,128)}) custom-call(s32[3]{0:T(128)} %pad_add_fusion.info_ref, f32[256,1024]{1,0:T(8,128)} %get-tuple-element.7.k_ref, f32[1024,1024]{1,0:T(8,128)} %get-tuple-element.8.m_ref), custom_call_target="tpu_custom_call" | custom-call | flops 99999997952 | bytes 16777216 | tf_op jit(solution)/shard_map/factor_kernel/pallas_call | solution.py:472
  175.6 0.0 all-gather.5.cloned.1.call-done
  175.6 19.6 %next_kernel.1.nl_ref = f32[256,1024]{1,0:T(8,128)} custom-call(s32[3]{0:T(128)} %pad_add_fusion.info_ref, s32[128]{0:T(128)} %select_reduce_fusion.src_ref, bf16[256,3072]{1,0:T(8,128)(2,1)} %x_ref.3, f32[256,128]{1,0:T(8,128)} %broadcast_in_dim.32.q_ref, bf16[128,8,3072]{2,1,0:T(8,128)(2,1)} %bitcast.18), custom_call_target="tpu_custom_call" | custom-call | flops 20000000000 | bytes 16777216 | tf_op jit(solution)/shard_map/next_kernel/pallas_call | solution.py:482
  195.2 0.0 all-gather.3.cloned.1.call-done
  195.2 14.9 %update_kernel.1 = f32[256,1024]{1,0:T(8,128)} custom-call(s32[3]{0:T(128)} %pad_add_fusion.info_ref, s32[128]{0:T(128)} %select_reduce_fusion.src_ref, f32[256,1024]{1,0:T(8,128)} %get-tuple-element.5.f_ref, f32[1024,1024]{1,0:T(8,128)} %get-tuple-element.10.a_ref, f32[8,128,128]{2,1,0:T(8,128)} %get-tuple-element.11.inv_ref, f32[128,8,1024]{2,1,0:T(8,128)} %bitcast.19, ...), custom_call_target="tpu_custom_call" | custom-call | flops 10000000000 | bytes 16777216 | tf_op jit(solution)/shard_map/update_kernel/pallas_call | solution.py:492
  (1 shorter events, 0.0 us)
Async XLA Ops:
  7.2 46.2 %copy-start = (bf16[256,3072]{1,0:T(8,128)(2,1)S(1)}, bf16[256,3072]{1,0:T(8,128)(2,1)}, u32[]{:S(2)}) copy-start(bf16[256,3072]{1,0:T(8,128)(2,1)} %x_ref.3) | copy-start | bytes 4718596
  7.2 168.4 %all-gather.5.cloned.1.call-start = ((), (), s32[]{:S(2)}) async-start(), calls=%async_computation.1 | async-start | bytes 6340608 | tf_op jit(solution)/shard_map/all_gather | solution.py:444
  9.5 185.7 %all-gather.3.cloned.1.call-start = ((), (), s32[]{:S(2)}) async-start(), calls=%async_computation | async-start | bytes 4227072 | tf_op jit(solution)/shard_map/all_gather | solution.py:444
Sparse Core Ops, SparseCore 0:
  11.0 71.9 all-gather.4
  115.5 64.1 all-gather.2

commit v3 on v2

--- a/solution.py
+++ b/solution.py
@@ -19,14 +19,10 @@
 f32 = jnp.float32
 bf16 = jnp.bfloat16
 
-ARC = (
-    0.30010470747947693,
-    0.015018727630376816,
-    0.0023307923693209887,
-    0.0007760883891023695,
-    -0.00012745900312438607,
-    0.00020702359324786812,
-)
+ARC_A = 0.2353731889436501
+ARC_B = 0.116208962721599
+ARC_C = 3.2233309496295237
+ARC_D = 0.005000674198862276
 
 
 def nn(a, b):
@@ -101,11 +97,10 @@
     ]
     for n in range(DEPTH):
         for w in range(pieces):
-            u = jnp.maximum(1.0 - jnp.abs(c[w]), 1e-30)
-            p = ARC[5] * u + ARC[4]
-            for k in (3, 2, 1, 0):
-                p = p * u + ARC[k]
-            g = jnp.maximum(c[w], 0.0) + (u * u) * lax.rsqrt(u) * p
+            size = jnp.abs(c[w]) if n == 0 else c[w]
+            u = jnp.maximum(1.0 - size, 1e-30)
+            p = (ARC_D * u + ARC_A) + ARC_B * lax.rsqrt(ARC_C - u)
+            g = (jnp.maximum(c[w], 0.0) if n == 0 else c[w]) + (u * u) * lax.rsqrt(u) * p
             if n < DEPTH - 1:
                 c[w] = g * (ratio[n] * col(1 + n, w)) + offset[n] * col(DEPTH + n, w)
             else:
@@ -113,50 +108,71 @@
     return jnp.concatenate(c, axis=1)
 
 
-def block_inverse(d_ref):
+def total(xs):
+    xs = list(xs)
+    while len(xs) > 1:
+        xs = [xs[i] + xs[i + 1] if i + 1 < len(xs) else xs[i] for i in range(0, len(xs), 2)]
+    return xs[0]
+
+
+def block_inverse(d_ref, cs_ref):
     lane = lax.broadcasted_iota(jnp.int32, (8, TILE), 1)
     sub = lax.broadcasted_iota(jnp.int32, (8, TILE), 0)
     spread = lambda x: jnp.broadcast_to(x, (8, TILE))
+    now = d_ref[0:8, :]
     for s in range(TILE // 8):
         r0 = 8 * s
+        slot = 64 * (s % 2)
         inside = (lane >= r0) & (lane < r0 + 8)
-        rows = [spread(d_ref[r0 + j : r0 + j + 1, :]) for j in range(8)]
+        for j in range(8):
+            cs_ref[slot + 8 * j : slot + 8 * j + 8, :] = spread(now[:, r0 + j : r0 + j + 1])
         e = [
-            [spread(rows[i][:, r0 + j : r0 + j + 1]) if j >= i else None for j in range(8)]
+            [
+                spread(cs_ref[slot + 8 * j + i : slot + 8 * j + i + 1, :]) if j >= i else None
+                for j in range(8)
+            ]
             for i in range(8)
         ]
         below = {}
         for i in range(s + 1, TILE // 8):
             b = d_ref[8 * i : 8 * i + 8, :]
             below[i] = (b, [spread(b[:, r0 + j : r0 + j + 1]) for j in range(8)])
-        u = [jnp.where(inside, (lane == r0 + j).astype(f32), rows[j]) for j in range(8)]
-        ys, rs = [], []
-        for j in range(8):
-            y = lax.rsqrt(e[j][j])
-            r = y * y
-            ys.append(y)
-            rs.append(r)
-            for i in range(j + 1, 8):
-                f = e[j][i] * r
+        t = [
+            jnp.where(inside, (lane == r0 + j).astype(f32), spread(d_ref[r0 + j : r0 + j + 1, :]))
+            for j in range(8)
+        ]
+        w = [[None] * 8 for _ in range(8)]
+        z = [None] * 8
+        rows = [None] * 8
+        for j in range(0, 8, 2):
+            a, b, c = e[j][j], e[j][j + 1], e[j + 1][j + 1]
+            root_det = lax.rsqrt(a * c - b * b)
+            root_a = lax.rsqrt(a)
+            rd = root_det * root_det
+            for i in range(j + 2, 8):
+                f0 = (c * e[j][i] - b * e[j + 1][i]) * rd
+                f1 = (a * e[j + 1][i] - b * e[j][i]) * rd
                 for q in range(i, 8):
-                    e[i][q] = e[i][q] - f * e[j][q]
-                u[i] = u[i] - f * u[j]
-        out = u[7] * ys[7]
+                    e[i][q] = e[i][q] - (f0 * e[j][q] + f1 * e[j + 1][q])
+                t[i] = t[i] - (f0 * t[j] + f1 * t[j + 1])
+                for k in range(j):
+                    w[i][k] = w[i][k] - (f0 * w[j][k] + f1 * w[j + 1][k])
+                w[i][j], w[i][j + 1] = -f0, -f1
+            z[j] = (c * t[j] - b * t[j + 1]) * rd
+            z[j + 1] = (a * t[j + 1] - b * t[j]) * rd
+            rows[j] = t[j] * root_a
+            rows[j + 1] = (t[j + 1] - (b * (root_a * root_a)) * t[j]) * (root_det * (a * root_a))
+        g = [total([z[k]] + [w[i][k] * z[i] for i in range(k // 2 * 2 + 2, 8)]) for k in range(8)]
+        out = rows[7]
         for j in range(6, -1, -1):
-            out = jnp.where(sub == j, u[j] * ys[j], out)
-        g = [None] * 8
-        for j in range(7, -1, -1):
-            acc = u[j] * rs[j]
-            for i in range(j + 1, 8):
-                acc = acc - (e[j][i] * rs[j]) * g[i]
-            g[j] = acc
+            out = jnp.where(sub == j, rows[j], out)
         d_ref[r0 : r0 + 8, :] = out
         for i in range(s + 1, TILE // 8):
             b, c = below[i]
-            acc = jnp.where(inside, 0.0, b)
-            for j in range(8):
-                acc = acc - c[j] * g[j]
+            acc = jnp.where(inside, 0.0, b) - total([c[j] * g[j] for j in range(8)])
             d_ref[8 * i : 8 * i + 8, :] = acc
+            if i == s + 1:
+                now = acc
 
 
 def place_points(src_ref, raw_ref, p_ref):
@@ -194,13 +210,21 @@
     lax.fori_loop(start, out_ref.shape[0] // GROUP, row_block, 0)
 
 
-def panel_kernel(info_ref, src_ref, x_ref, q_ref, raw_ref, out_ref, a_ref, p_ref, tab_ref, qrow_ref):
+def cross_kernel(info_ref, src_ref, x_ref, q_ref, raw_ref, out_ref, p_ref, tab_ref, *, after):
+    place_points(src_ref, raw_ref, p_ref)
+    for b in range(STEPS):
+        store_columns(tab_ref, b * TILE, own_square(p_ref, b * TILE)[0])
+    local_kernel(info_ref, x_ref, q_ref, p_ref, out_ref, tab_ref, after)
+
+
+def factor_kernel(
+    info_ref, src_ref, raw_ref, k_ref, f_ref, g_ref, p_ref, a_ref, inv_ref, tab_ref, qrow_ref, d_ref, cs_ref
+):
     place_points(src_ref, raw_ref, p_ref)
     for b in range(STEPS):
         along, down = own_square(p_ref, b * TILE)
         store_columns(tab_ref, b * TILE, along)
         qrow_ref[b * TILE : (b + 1) * TILE, :] = jnp.broadcast_to(down, (TILE, TILE))
-    local_kernel(info_ref, x_ref, q_ref, p_ref, out_ref, tab_ref, 0)
     for b in range(PANEL // 256):
         lo = b * 256
         for c in range(b, PANEL // 256):
@@ -219,16 +243,6 @@
 
         lax.fori_loop(lo // GROUP, (lo + 256) // GROUP, row_block, 0)
 
-
-def next_kernel(info_ref, src_ref, x_ref, q_ref, raw_ref, out_ref, p_ref, tab_ref):
-    place_points(src_ref, raw_ref, p_ref)
-    for b in range(STEPS):
-        store_columns(tab_ref, b * TILE, own_square(p_ref, b * TILE)[0])
-    local_kernel(info_ref, x_ref, q_ref, p_ref, out_ref, tab_ref, 1)
-
-
-def factor_kernel(info_ref, k_ref, m_ref, f_ref, a_ref, inv_ref, d_ref):
-    a_ref[...] = m_ref[...]
     row = lax.broadcasted_iota(jnp.int32, (TILE, TILE), 0)
     col = lax.broadcasted_iota(jnp.int32, (TILE, TILE), 1)
     f_ref[...] = k_ref[...]
@@ -236,7 +250,7 @@
     def step(k, carry):
         k0 = pl.multiple_of(k * TILE, TILE)
         d_ref[...] = a_ref[pl.ds(k0, TILE), pl.ds(k0, TILE)]
-        block_inverse(d_ref)
+        block_inverse(d_ref, cs_ref)
         linv = jnp.where(row >= col, d_ref[...], 0.0)
         inv_ref[k] = linv
         for kk in range(STEPS - 1):
@@ -270,14 +284,6 @@
     within = lax.broadcasted_iota(jnp.int32, (GROUP, PANEL), 0)
     f_ref[at, :] = jnp.where(column <= info_ref[1] * GROUP + within, f_ref[at, :], 0.0)
 
-
-def update_kernel(info_ref, src_ref, f_ref, a_ref, inv_ref, nk_ref, nl_ref, out_ref, g_ref, kn_ref):
-    def place(b, carry):
-        at = pl.ds(pl.multiple_of(b * GROUP, GROUP), GROUP)
-        kn_ref[at, :] = nk_ref[src_ref[b]]
-        return carry
-
-    lax.fori_loop(0, PANEL // GROUP, place, 0, unroll=8)
     for k in range(STEPS - 1, -1, -1):
         b0, c0 = k * TILE, (k + 1) * TILE
         x = f_ref[:, b0:c0]
@@ -285,7 +291,16 @@
             j0 = j * TILE
             x = x - nt(lhs6(g_ref[:, j0 : j0 + TILE]), rhs6_nt(a_ref[b0:c0, j0 : j0 + TILE]))
         g_ref[:, b0:c0] = nn(lhs6(x), rhs6_nn(inv_ref[k]))
-    rows = lax.broadcasted_iota(jnp.int32, (f_ref.shape[0], 256), 0) // GROUP
+
+
+def update_kernel(info_ref, src_ref, g_ref, nk_ref, nl_ref, out_ref, kn_ref):
+    def place(b, carry):
+        at = pl.ds(pl.multiple_of(b * GROUP, GROUP), GROUP)
+        kn_ref[at, :] = nk_ref[src_ref[b]]
+        return carry
+
+    lax.fori_loop(0, PANEL // GROUP, place, 0, unroll=8)
+    rows = lax.broadcasted_iota(jnp.int32, (g_ref.shape[0], 256), 0) // GROUP
     live = rows > info_ref[0]
     for b in range(PANEL // 256):
         total = nl_ref[:, b * 256 : (b + 1) * 256]
@@ -456,49 +471,50 @@
     table = pltpu.VMEM((24, PANEL), f32)
     placed = pltpu.VMEM((PANEL, features), bf16)
     rows_out = jax.ShapeDtypeStruct((rows_dev, PANEL), f32)
-    square = jax.ShapeDtypeStruct((PANEL, PANEL), f32)
-
-    matrix, diagonal = pl.pallas_call(
-        panel_kernel,
-        out_shape=(rows_out, square),
-        in_specs=[SMEM, SMEM, VMEM, VMEM, VMEM],
+
+    def cross(blocks, order, after):
+        return pl.pallas_call(
+            lambda *refs: cross_kernel(*refs, after=after),
+            out_shape=rows_out,
+            in_specs=[SMEM, SMEM, VMEM, VMEM, VMEM],
+            out_specs=VMEM,
+            scratch_shapes=[placed, table],
+            compiler_params=PARAMS,
+            name="cross_kernel",
+            cost_estimate=pl.CostEstimate(flops=2 * 10**10, bytes_accessed=16 << 20, transcendentals=0),
+        )(info, order, images, local_var, blocks)
+
+    matrix = cross(points, sources, 0)
+    next_rows = gather(own(panel + 1, matrix))
+    factor, weights = pl.pallas_call(
+        factor_kernel,
+        out_shape=(rows_out, rows_out),
+        in_specs=[SMEM, SMEM, VMEM, VMEM],
         out_specs=(VMEM, VMEM),
-        scratch_shapes=[placed, table, pltpu.VMEM((PANEL, TILE), f32)],
-        compiler_params=PARAMS,
-        name="panel_kernel",
-        cost_estimate=pl.CostEstimate(flops=3 * 10**10, bytes_accessed=16 << 20, transcendentals=0),
-    )(info, sources, images, local_var, points)
-    next_rows = gather(own(panel + 1, matrix))
-    factor, upper, inverses = pl.pallas_call(
-        factor_kernel,
-        out_shape=(rows_out, square, jax.ShapeDtypeStruct((STEPS, TILE, TILE), f32)),
-        in_specs=[SMEM, VMEM, VMEM],
-        out_specs=(VMEM, VMEM, VMEM),
-        scratch_shapes=[pltpu.VMEM((TILE, TILE), f32)],
+        scratch_shapes=[
+            placed,
+            pltpu.VMEM((PANEL, PANEL), f32),
+            pltpu.VMEM((STEPS, TILE, TILE), f32),
+            table,
+            pltpu.VMEM((PANEL, TILE), f32),
+            pltpu.VMEM((TILE, TILE), f32),
+            pltpu.VMEM((TILE, TILE), f32),
+        ],
         compiler_params=PARAMS,
         name="factor_kernel",
         cost_estimate=pl.CostEstimate(flops=10**11, bytes_accessed=16 << 20, transcendentals=0),
-    )(info, matrix, diagonal)
-    next_matrix = pl.pallas_call(
-        next_kernel,
+    )(info, sources, points, matrix)
+    next_matrix = cross(next_points, next_sources, 1)
+    updated = pl.pallas_call(
+        update_kernel,
         out_shape=rows_out,
         in_specs=[SMEM, SMEM, VMEM, VMEM, VMEM],
         out_specs=VMEM,
-        scratch_shapes=[placed, table],
-        compiler_params=PARAMS,
-        name="next_kernel",
-        cost_estimate=pl.CostEstimate(flops=2 * 10**10, bytes_accessed=16 << 20, transcendentals=0),
-    )(info, next_sources, images, local_var, next_points)
-    updated = pl.pallas_call(
-        update_kernel,
-        out_shape=jax.ShapeDtypeStruct((rows_dev, PANEL), f32),
-        in_specs=[SMEM, SMEM, VMEM, VMEM, VMEM, VMEM, VMEM],
-        out_specs=VMEM,
-        scratch_shapes=[pltpu.VMEM((rows_dev, PANEL), f32), pltpu.VMEM((PANEL, PANEL), f32)],
+        scratch_shapes=[pltpu.VMEM((PANEL, PANEL), f32)],
         compiler_params=PARAMS,
         name="update_kernel",
         cost_estimate=pl.CostEstimate(flops=10**10, bytes_accessed=16 << 20, transcendentals=0),
-    )(info, next_sources, factor, upper, inverses, next_rows, next_matrix)
+    )(info, next_sources, weights, next_rows, next_matrix)
     return (factor, updated)
 
 

time: 217 us -> 174 us (0.80)
  Pallas kernels: 193 us -> 151 us
    pallas_call x4, Pallas kernels: 154 us -> 111 us  [the longest x1 80.3 us: body(): pl.pallas_call(factor_kernel, out_shape=(rows_out, rows_out), in_specs=[S...]
  transfers between devices with their start and end apart: 2 -> 2, of which waited for: 0 -> 0; matrix products, arithmetic and copies ran while one was open for 3% -> 4% of each run, Pallas kernels for 82% -> 82%
where the time goes in v3:
time: 174 us
  Pallas kernels  151 us (87%)
  between operations  14.7 us (8%)
  other arithmetic  4.32 us (2%)
  local copies, waits for them, and re-layouts  4.26 us (2%)
    pallas_call x1, Pallas kernels, body(): pl.pallas_call(factor_kernel, out_shape=(rows_out, rows_out), in_specs=[S...  80.3 us
    pallas_call x1, Pallas kernels, gather_blocks(): pl.pallas_call(lambda *refs: gather_kernel(*refs, cuts=cuts), out_shape=j...  40 us
    pallas_call x2, Pallas kernels, cross(): pl.pallas_call(lambda *refs: cross_kernel(*refs, after=after), out_shape=...  22.2 us
    pallas_call x1, Pallas kernels, body(): pl.pallas_call(update_kernel, out_shape=rows_out, in_specs=[SMEM, SMEM, V...  8.04 us
  transfers between devices with their start and end apart: 2, of which 0 were waited for; matrix products, arithmetic and copies ran while one was open for 4% of the time, Pallas kernels for 82%

profile of v3, /device:TPU:1, one launch (start us, length us, event | category | flops | bytes accessed | tf_op | source)
XLA Modules:
  0.0 174.0 jit_solution(7240593658323276065)
XLA Ops:
  7.2 0.0 all-gather.5.cloned.1.call-start
  7.9 1.5 constant_dynamic-slice_fusion
  9.3 0.0 all-gather.5.cloned.1.call-update
  9.4 0.0 all-gather.3.cloned.1.call-start
  9.4 0.0 copy-start
  9.4 40.0 %gather_kernel.1 = bf16[4,4,2,4,8,3072]{5,4,3,2,1,0:T(8,128)(2,1)} custom-call(bf16[8,3072]{1,0:T(8,128)(2,1)} %get-tuple-element.7.refs_0_), custom_call_target="tpu_custom_call" | custom-call | tf_op jit(solution)/shard_map/gather_kernel/pallas_call | solution.py:415
  49.4 0.7 fusion
  50.2 0.7 constant_dynamic-slice_fusion.3
  50.8 1.9 %pad_add_fusion.refs_0_.info_ref = s32[3]{0:T(128)} fusion(s32[1]{0:T(128)} %bitcast.2, s32[1]{0:T(128)} %bitcast.1, s32[1]{0:T(128)} %copy.5), kind=kLoop, calls=%fused_computation.15 | loop fusion | flops 6 | bytes 24 | tf_op jit(solution)/shard_map/stack | solution.py:468
  52.8 0.6 select_reduce_fusion.1.refs_1_.src_ref
  53.4 0.0 copy-done
  53.4 0.4 multiply_reduce_fusion
  53.8 0.8 broadcast_in_dim.32.refs_3_
  54.5 11.2 %cross_kernel.2.k_ref = f32[256,1024]{1,0:T(8,128)} custom-call(s32[3]{0:T(128)} %pad_add_fusion.refs_0_.info_ref, s32[128]{0:T(128)} %select_reduce_fusion.1.refs_1_.src_ref, bf16[256,3072]{1,0:T(8,128)(2,1)} %refs_2_.3, f32[256,128]{1,0:T(8,128)} %broadcast_in_dim.32.refs_3_, bf16[128,8,3072]{2,1,0:T(8,128)(2,1)} %bitcast.15), custom_call_target="tpu_custom_call" | custom-call | flops 20000000000 | bytes 16777216 | tf_op jit(solution)/shard_map/cross_kernel/pallas_call | solution.py:476
  65.7 1.4 constant_dynamic-slice_fusion.1
  67.1 0.0 all-gather.3.cloned.1.call-update
  67.1 0.7 select_reduce_fusion.refs_1_.src_ref
  67.8 80.3 %factor_kernel.1 = (f32[256,1024]{1,0:T(8,128)}, f32[256,1024]{1,0:T(8,128)}) custom-call(s32[3]{0:T(128)} %pad_add_fusion.refs_0_.info_ref, s32[128]{0:T(128)} %select_reduce_fusion.1.refs_1_.src_ref, bf16[128,8,3072]{2,1,0:T(8,128)(2,1)} %bitcast.16, f32[256,1024]{1,0:T(8,128)} %cross_kernel.2.k_ref), custom_call_target="tpu_custom_call" | custom-call | flops 99999997952 | bytes 16777216 | tf_op jit(solution)/shard_map/factor_kernel/pallas_call | solution.py:489
  148.1 0.0 all-gather.5.cloned.1.call-done
  148.1 11.0 %cross_kernel.3.nl_ref = f32[256,1024]{1,0:T(8,128)} custom-call(s32[3]{0:T(128)} %pad_add_fusion.refs_0_.info_ref, s32[128]{0:T(128)} %select_reduce_fusion.refs_1_.src_ref, bf16[256,3072]{1,0:T(8,128)(2,1)} %refs_2_.3, f32[256,128]{1,0:T(8,128)} %broadcast_in_dim.32.refs_3_, bf16[128,8,3072]{2,1,0:T(8,128)(2,1)} %bitcast.19), custom_call_target="tpu_custom_call" | custom-call | flops 20000000000 | bytes 16777216 | tf_op jit(solution)/shard_map/cross_kernel/pallas_call | solution.py:476
  159.1 0.0 all-gather.3.cloned.1.call-done
  159.1 8.0 %update_kernel.1 = f32[256,1024]{1,0:T(8,128)} custom-call(s32[3]{0:T(128)} %pad_add_fusion.refs_0_.info_ref, s32[128]{0:T(128)} %select_reduce_fusion.refs_1_.src_ref, f32[256,1024]{1,0:T(8,128)} %get-tuple-element.5.g_ref, f32[128,8,1024]{2,1,0:T(8,128)} %bitcast.20, f32[256,1024]{1,0:T(8,128)} %cross_kernel.3.nl_ref), custom_call_target="tpu_custom_call" | custom-call | flops 10000000000 | bytes 16777216 | tf_op jit(solution)/shard_map/update_kernel/pallas_call | solution.py:508
  (1 shorter events, 0.0 us)
Async XLA Ops:
  7.2 140.9 %all-gather.5.cloned.1.call-start = ((), (), s32[]{:S(2)}) async-start(), calls=%async_computation.1 | async-start | bytes 6340608 | tf_op jit(solution)/shard_map/all_gather | solution.py:459
  9.4 149.7 %all-gather.3.cloned.1.call-start = ((), (), s32[]{:S(2)}) async-start(), calls=%async_computation | async-start | bytes 4227072 | tf_op jit(solution)/shard_map/all_gather | solution.py:459
  9.4 43.9 %copy-start = (bf16[256,3072]{1,0:T(8,128)(2,1)S(1)}, bf16[256,3072]{1,0:T(8,128)(2,1)}, u32[]{:S(2)}) copy-start(bf16[256,3072]{1,0:T(8,128)(2,1)} %refs_2_.3) | copy-start | bytes 4718596
Sparse Core Ops, SparseCore 0:
  11.0 71.9 all-gather.4
  86.2 64.5 all-gather.2
